TPU v7x, 128 devices: a whole 4x4x4 slice. The times are simulated.
128 devices in a mesh: section: 8 (over x, z_hi), ctx: 16 (over z_lo, y, core).
Axes of the slice: x: 4, y: 4, z: 4 (z_hi: 2, z_lo: 2; z = z_hi * 2 + z_lo), core: 2. Of those that a mesh axis runs over, the one named last changes fastest.
Arguments:
- acts: bfloat16 [8, 2048, 12288], P('section', 'ctx'), may hold values from -6 to 6
- cots: bfloat16 [8, 2048, 4096], P('section', 'ctx'), may hold values from -1.1953125 to 1.1953125
- kern: float32 [8, 7, 12288], P('section'), may hold values from -2 to 2
- filt: bfloat16 [8, 4096, 2048], P('section', 'ctx'), may hold values from -9 to 9
- skip: float32 [8, 4096], P('section'), may hold values from 0.5 to 1.5
Outputs:
- output: bfloat16 [8, 2048, 4096], P('section', 'ctx')
- input_grad: bfloat16 [8, 2048, 12288], P('section', 'ctx')
- kern_grad: float32 [8, 7, 12288], P('section')
- filt_grad: float32 [8, 4096, 2048], P('section', 'ctx')
- skip_grad: float32 [8, 4096], P('section', 'ctx')
All inputs are finite; a program needn't handle non-finite values.
Results may differ from a plain program's by a relative error of at most 0.023.
Values may be sent and summed in bfloat16 or wider, within the bound.
No kernel may reach another device: no remote copies, remote signals or barrier semaphores. Data moves between devices by JAX's collectives and lax.ppermute only.
A program may use at most 192 MiB of HBM per device.

v0:
```python
import math
import jax
import jax.numpy as jnp
from jax import lax
from jax.sharding import PartitionSpec as P


def passed_along(value, axis, steps):
    count = lax.axis_size(axis)
    pairs = [(source, (source + steps) % count) for source in range(count)]
    return lax.ppermute(value, axis, pairs)


def from_behind(block, axis, distance):
    devices = range(lax.axis_size(axis))
    route = [(i - distance, i) for i in devices if i - distance in devices]
    return lax.ppermute(block, axis, route)


def factor_length(total):
    best = 2
    for divisor in range(2, math.isqrt(total) + 1):
        if total % divisor == 0 and divisor % 2 == 0:
            best = divisor
    return (best, total // best)


def phases(rows, cols, total):
    left = jnp.arange(rows, dtype=jnp.int32)[:, None]
    right = jnp.arange(cols, dtype=jnp.int32)[None, :]
    return (left * right % total).astype(jnp.float32) * (2.0 * math.pi / total)


def block_table(cos_t, sin_t, sign):
    top = jnp.stack([cos_t, sign * sin_t], axis=1)
    bottom = jnp.stack([-sign * sin_t, cos_t], axis=1)
    return jnp.stack([top, bottom], axis=0)


def make_tables(first, second):
    total = first * second
    outer = phases(first, first // 2, first)
    twist = phases(first, second, total)
    inner = phases(second, second, second)
    outer_pair = jnp.stack([jnp.cos(outer), -jnp.sin(outer)], axis=0)
    inner_cos = jnp.cos(inner)
    inner_sin = jnp.sin(inner)
    return (
        outer_pair,
        jnp.cos(twist),
        jnp.sin(twist),
        block_table(inner_cos, inner_sin, 1.0),
        block_table(inner_cos, inner_sin, -1.0),
    )


def contract(form, table, values):
    return jnp.einsum(form, table, values, precision=lax.Precision.HIGH)


def contract_narrow(form, table, values):
    upper = table.astype(jnp.bfloat16)
    lower = (table - upper.astype(jnp.float32)).astype(jnp.bfloat16)
    return jnp.einsum(form, upper, values, preferred_element_type=jnp.float32) + jnp.einsum(
        form, lower, values, preferred_element_type=jnp.float32
    )


def forward_transform(signal, tables):
    outer_pair, twist_cos, twist_sin, inner_fwd, inner_inv = tables
    first, second = twist_cos.shape
    columns = signal.shape[1]
    blocked = signal.reshape(first // 2, second, columns)
    spread = contract_narrow("pkm,mjc->pkjc", outer_pair, blocked)
    a_real = spread[0]
    a_imag = spread[1]
    b_real = a_real * twist_cos[:, :, None] + a_imag * twist_sin[:, :, None]
    b_imag = a_imag * twist_cos[:, :, None] - a_real * twist_sin[:, :, None]
    stacked = jnp.stack([b_real, b_imag], axis=0)
    return contract("pqsj,skjc->pkqc", inner_fwd, stacked)


def cmul(left, right, conj_right):
    if conj_right:
        return jnp.stack(
            [left[0] * right[0] + left[1] * right[1], left[1] * right[0] - left[0] * right[1]],
            axis=0,
        )
    return jnp.stack(
        [left[0] * right[0] - left[1] * right[1], left[0] * right[1] + left[1] * right[0]], axis=0
    )


def inverse_transform(spectrum, tables):
    outer_pair, twist_cos, twist_sin, inner_fwd, inner_inv = tables
    first, second = twist_cos.shape
    columns = spectrum.shape[3]
    back = contract("pjsq,skqc->pkjc", inner_inv, spectrum)
    g_real = back[0] * twist_cos[:, :, None] - back[1] * twist_sin[:, :, None]
    g_imag = back[0] * twist_sin[:, :, None] + back[1] * twist_cos[:, :, None]
    result = contract("skm,skjc->mjc", outer_pair, jnp.stack([g_real, g_imag], axis=0))
    return result.reshape(first // 2 * second, columns) / (first * second)


def on_device(acts, cots, kern, filt, skip):
    source = passed_along(acts, "section", 1)[0]
    incoming = passed_along(cots, "section", -1)[0]
    taps = kern.shape[1]
    margin = taps - 1
    tokens_dev, feats = source.shape
    width = feats // 3
    groups = lax.axis_size("ctx")
    chans = width // groups
    seq_len = tokens_dev * groups
    before = from_behind(source[tokens_dev - margin :], "ctx", 1)
    padded = jnp.concatenate([before, source], axis=0).astype(jnp.float32)
    weights = kern[0]
    feature = sum(
        (
            weights[offset][None, :] * padded[margin - offset : margin - offset + tokens_dev]
            for offset in range(taps)
        )
    )
    query = feature[:, :width]
    keyed = feature[:, width : 2 * width]
    value = feature[:, 2 * width :]
    gated = (keyed * value).astype(jnp.bfloat16)
    gain_all = skip[0]
    gain_part = lax.dynamic_slice_in_dim(gain_all, lax.axis_index("ctx") * chans, chans)
    first, second = factor_length(2 * seq_len)
    tables = make_tables(first, second)
    filt_spec = forward_transform(filt[0].T, tables)
    grad_in = incoming.astype(jnp.float32)
    grad_mix = (grad_in * query).astype(jnp.bfloat16)
    gated_part = lax.all_to_all(gated, "ctx", split_axis=1, concat_axis=0, tiled=True)
    gated_f = gated_part.astype(jnp.float32)
    gated_spec = forward_transform(gated_part, tables)
    mixed = inverse_transform(cmul(gated_spec, filt_spec, False), tables)
    mixed_part = mixed.astype(jnp.bfloat16)
    mixed_seq = lax.all_to_all(mixed_part, "ctx", split_axis=0, concat_axis=1, tiled=True)
    grad_part = lax.all_to_all(grad_mix, "ctx", split_axis=1, concat_axis=0, tiled=True)
    gated_f, gated_spec = (gated_f, gated_spec)
    grad_f = grad_part.astype(jnp.float32)
    grad_spec = forward_transform(grad_part, tables)
    back = inverse_transform(cmul(grad_spec, filt_spec, True), tables)
    filt_grad = inverse_transform(cmul(grad_spec, gated_spec, True), tables)
    through = (back + gain_part[None, :] * grad_f).astype(jnp.bfloat16)
    skip_grad = jnp.sum(grad_f * gated_f, axis=0)
    through_part, filt_grad, skip_grad = (through, filt_grad, skip_grad)
    through_seq = lax.all_to_all(through_part, "ctx", split_axis=0, concat_axis=1, tiled=True)
    inner = mixed_seq.astype(jnp.float32) + gain_all[None, :] * gated.astype(jnp.float32)
    output = (query * inner).astype(jnp.bfloat16)
    through_f = through_seq.astype(jnp.float32)
    feat_grad = jnp.concatenate([grad_in * inner, through_f * value, through_f * keyed], axis=1)
    after = from_behind(feat_grad[:margin].astype(jnp.bfloat16), "ctx", -1).astype(jnp.float32)
    extended = jnp.concatenate([feat_grad, after], axis=0)
    input_grad = sum(
        (
            weights[offset][None, :] * extended[offset : offset + tokens_dev]
            for offset in range(taps)
        )
    ).astype(jnp.bfloat16)
    partial_kern = jnp.sum(
        jnp.stack(
            [
                feat_grad * padded[margin - offset : margin - offset + tokens_dev]
                for offset in range(taps)
            ],
            axis=0,
        ),
        axis=1,
    )
    kern_grad = lax.psum(partial_kern.astype(jnp.bfloat16), "ctx").astype(jnp.float32)
    return (output[None], input_grad[None], kern_grad[None], filt_grad.T[None], skip_grad[None])


def solution(mesh):
    return jax.shard_map(
        on_device,
        mesh=mesh,
        in_specs=(
            P("section", "ctx", None),
            P("section", "ctx", None),
            P("section", None, None),
            P("section", "ctx", None),
            P("section", None),
        ),
        out_specs=(
            P("section", "ctx", None),
            P("section", "ctx", None),
            P("section", None, None),
            P("section", "ctx", None),
            P("section", "ctx"),
        ),
        check_vma=False,
    )
```

profile of v0, /device:TPU:25, one launch (start us, length us, event | category | flops | bytes accessed | tf_op | source)
XLA Modules:
  0.0 614.9 jit_solution(2262165847482371102)
XLA Ops:
  22.4 82.2 %collective-permute-done = bf16[1,128,12288]{1,2,0:T(8,128)(2,1)} collective-permute-done((bf16[1,128,12288]{1,2,0:T(8,128)(2,1)}, bf16[1,128,12288]{1,2,0:T(8,128)(2,1)}, u32[]{:S(2)}, u32[]{:S(2)}) %collective-permute-start) | collective-permute-done | bytes 3145760 | tf_op jit(solution)/shard_map/ppermute | solution.py:11
  126.1 24.5 %multiply_add_fusion = f32[128,12288]{0,1:T(8,128)} fusion(f32[134,12288]{0,1:T(8,128)S(1)} %maximum_convert_fusion, f32[12288]{0:T(1024)S(1)} %bitcast.243, f32[12288]{0:T(1024)S(1)} %bitcast.245, f32[12288]{0:T(1024)S(1)} %bitcast.235, f32[12288]{0:T(1024)S(1)} %bitcast.237, f32[12288]{0:T(1024)S(1)} %bitcast.239, f32[12288]{0:T(1024)S(1)} %bitcast.241, ...), kind=kLoop, calls=%fused_computation.60 | loop fusion | flops 20447232 | bytes 50675712 | tf_op jit(solution)/shard_map/add | solution.py:118
  153.8 7.0 %all-to-all-start.2 = ((bf16[128,16,256]{0,2,1:T(8,128)(2,1)}), bf16[128,16,256]{0,2,1:T(8,128)(2,1)S(1)}, u32[]{:S(2)}, u32[]{:S(2)}) async-start(bf16[128,16,256]{0,2,1:T(8,128)(2,1)} %bitcast.232), calls=%async_computation.2 | async-start | bytes 2097152 | tf_op jit(solution)/shard_map/all_to_all | solution.py:141
  166.7 7.9 %all-to-all-done.2 = bf16[128,16,256]{0,2,1:T(8,128)(2,1)S(1)} async-done(((bf16[128,16,256]{0,2,1:T(8,128)(2,1)}), bf16[128,16,256]{0,2,1:T(8,128)(2,1)S(1)}, u32[]{:S(2)}, u32[]{:S(2)}) %all-to-all-start.2) | async-done | bytes 1048608 | tf_op jit(solution)/shard_map/all_to_all | solution.py:141
  178.8 7.3 %multiply_add_fusion.5 = (f32[1,64,64,256]{3,1,2,0:T(8,128)}, f32[1,64,64,256]{3,1,2,0:T(8,128)}, f32[1,64,64,256]{3,1,2,0:T(8,128)}, f32[1,64,64,256]{3,1,2,0:T(8,128)}) fusion(f32[2,64,64,256]{3,1,2,0:T(8,128)S(1)} %convolution_add_fusion, f32[64,64]{0,1:T(8,128)S(1)} %get-tuple-element.64, f32[64,64]{0,1:T(8,128)S(1)} %get-tuple-element.65, ...), kind=kLoop, calls=%fused_computation.70 | loop fusion | flops 12582912 | bytes 33587200 | tf_op jit(solution)/shard_map/add | solution.py:77
  194.3 8.5 %fusion.40 = f32[2,64,64,256]{3,2,0,1:T(8,128)S(1)} fusion(f32[2,64,64,256,1]{3,1,2,0,4:T(8,128)S(1)} %maximum_bitcast_fusion.4, f32[1,64,2,64]{3,1,2,0:T(8,128)S(1)} %get-tuple-element.57, f32[1,64,2,64]{3,1,2,0:T(8,128)S(1)} %get-tuple-element.60), kind=kOutput, calls=%fused_computation.84 | convolution fusion | flops 1610629120 | bytes 16842752 | tf_op jit(solution)/shard_map/pqsj,skjc->pkqc/dot_general | solution.py:58
  202.8 8.7 %fusion.37 = f32[2,64,64,256]{3,2,0,1:T(8,128)S(1)} fusion(f32[2,64,64,256,1]{3,1,2,0,4:T(8,128)S(1)} %maximum_bitcast_fusion.1, f32[1,64,2,64]{3,1,2,0:T(8,128)S(1)} %get-tuple-element.57, f32[1,64,2,64]{3,1,2,0:T(8,128)S(1)} %get-tuple-element.60), kind=kOutput, calls=%fused_computation.83 | convolution fusion | flops 1610629120 | bytes 16842752 | tf_op jit(solution)/shard_map/pqsj,skjc->pkqc/dot_general | solution.py:58
  238.0 19.4 %all_to_all.52 = bf16[16,128,256]{1,2,0:T(8,128)(2,1)S(1)} all-to-all(bf16[16,128,256]{1,2,0:T(8,128)(2,1)S(1)} %fusion.48), channel_id=1, replica_groups=mesh['section'=8,'ctx'=16] {'ctx'}, dimensions={0} | all-to-all | bytes 2097152 | tf_op jit(solution)/shard_map/all_to_all | solution.py:150
  262.3 20.2 %all_to_all.53 = bf16[128,16,256]{0,2,1:T(8,128)(2,1)} all-to-all(bf16[128,16,256]{0,2,1:T(8,128)(2,1)S(1)} %bitcast.220), channel_id=1, replica_groups=mesh['section'=8,'ctx'=16] {'ctx'}, dimensions={1} | all-to-all | bytes 2097152 | tf_op jit(solution)/shard_map/all_to_all | solution.py:135
  294.3 14.0 %fusion.34 = f32[2,64,64,256]{3,2,0,1:T(8,128)} fusion(f32[2,64,64,256,1]{3,1,2,0,4:T(8,128)} %maximum_bitcast_fusion, f32[1,64,2,64]{3,1,2,0:T(8,128)S(1)} %get-tuple-element.57, f32[1,64,2,64]{3,1,2,0:T(8,128)S(1)} %get-tuple-element.60), kind=kOutput, calls=%fused_computation.82 | convolution fusion | flops 1610629120 | bytes 16842752 | tf_op jit(solution)/shard_map/pqsj,skjc->pkqc/dot_general | solution.py:58
  308.3 11.9 %multiply_add_fusion.2 = (f32[1,64,64,256]{3,2,0,1:T(8,128)}, f32[1,64,64,256]{3,2,0,1:T(8,128)}, f32[1,64,64,256]{3,2,0,1:T(8,128)}, f32[1,64,64,256]{3,2,0,1:T(8,128)}) fusion(f32[2,64,64,256]{3,2,0,1:T(8,128)S(1)} %bitcast.212, f32[2,64,64,256]{3,2,0,1:T(8,128)} %fusion.34, f32[2,64,64,256]{3,2,0,1:T(8,128)} %copy-done.8), kind=kLoop, calls=%fused_computation.64 | loop fusion | flops 12582912 | bytes 41943040 | tf_op jit(solution)/shard_map/add | solution.py:86
  337.9 8.2 %copy.163 = f32[64,256,2,64]{1,0,3,2:T(8,128)} copy(f32[64,256,2,64]{1,3,2,0:T(8,128)S(1)} %fusion.43) | data formatting | bytes 16777216 | tf_op jit(solution)/shard_map/pjsq,skqc->pkjc/dot_general | solution.py:58
  346.1 7.9 %multiply_subtract_fusion = (f32[1,64,64,256]{3,1,2,0:T(8,128)}, f32[1,64,64,256]{3,1,2,0:T(8,128)}, f32[1,64,64,256]{3,1,2,0:T(8,128)S(1)}, f32[1,64,64,256]{3,1,2,0:T(8,128)}) fusion(f32[2,64,64,256]{3,1,2,0:T(8,128)} %bitcast.217, f32[64,64]{0,1:T(8,128)S(1)} %get-tuple-element.64, f32[64,64]{0,1:T(8,128)S(1)} %get-tuple-element.65, ...), kind=kLoop, calls=%fused_computation.62 | loop fusion | flops 12582912 | bytes 33587200 | tf_op jit(solution)/shard_map/sub | solution.py:99
  397.4 10.1 %bitcast_dynamic-update-slice_fusion.6 = f32[7,128,12288]{1,2,0:T(8,128)} fusion(f32[134,12288]{0,1:T(8,128)} %copy-done, f32[128,4096]{0,1:T(8,128)S(1)} %copy-done.1, f32[128,4096]{0,1:T(8,128)S(1)} %get-tuple-element.40, f32[128,4096]{0,1:T(8,128)S(1)} %get-tuple-element.43), kind=kLoop, calls=%fused_computation.59 | loop fusion | flops 4718591 | bytes 18874368
  412.9 10.0 %bitcast_dynamic-update-slice_fusion.5 = f32[7,128,12288]{1,2,0:T(8,128)} fusion(f32[7,128,12288]{1,2,0:T(8,128)} %bitcast_dynamic-update-slice_fusion.6, f32[134,12288]{0,1:T(8,128)} %copy-done, f32[128,4096]{0,1:T(8,128)} %get-tuple-element.41, f32[128,4096]{0,1:T(8,128)S(1)} %get-tuple-element.40, f32[128,4096]{0,1:T(8,128)} %copy-done.4), kind=kLoop, calls=%fused_computation.58 | loop fusion | flops 4718592 | bytes 18874368
  422.9 10.3 %bitcast_dynamic-update-slice_fusion.4 = f32[7,128,12288]{1,2,0:T(8,128)} fusion(f32[7,128,12288]{1,2,0:T(8,128)} %bitcast_dynamic-update-slice_fusion.5, f32[134,12288]{0,1:T(8,128)} %copy-done, f32[128,4096]{0,1:T(8,128)S(1)} %copy-done.2, f32[128,4096]{0,1:T(8,128)S(1)} %get-tuple-element.40, f32[128,4096]{0,1:T(8,128)S(1)} %copy-done.5), kind=kLoop, calls=%fused_computation.57 | loop fusion | flops 4718592 | bytes 18874368
  433.2 7.4 %bitcast_dynamic-update-slice_fusion.3 = f32[7,128,12288]{1,2,0:T(8,128)} fusion(f32[7,128,12288]{1,2,0:T(8,128)} %bitcast_dynamic-update-slice_fusion.4, f32[134,12288]{0,1:T(8,128)S(1)} %bitcast.210, f32[128,4096]{0,1:T(8,128)S(1)} %copy-done.2, f32[128,4096]{0,1:T(8,128)S(1)} %get-tuple-element.40, f32[128,4096]{0,1:T(8,128)S(1)} %copy-done.5), kind=kLoop, calls=%fused_computation.56 | loop fusion | flops 4718592 | bytes 18874368
  440.6 7.3 %bitcast_dynamic-update-slice_fusion.2 = f32[7,128,12288]{1,2,0:T(8,128)} fusion(f32[7,128,12288]{1,2,0:T(8,128)} %bitcast_dynamic-update-slice_fusion.3, f32[134,12288]{0,1:T(8,128)S(1)} %bitcast.210, f32[128,4096]{0,1:T(8,128)S(1)} %copy-done.2, f32[128,4096]{0,1:T(8,128)S(1)} %get-tuple-element.40, f32[128,4096]{0,1:T(8,128)S(1)} %copy-done.5), kind=kLoop, calls=%fused_computation.55 | loop fusion | flops 4718592 | bytes 18874368
  447.8 7.6 %bitcast_dynamic-update-slice_fusion.1 = f32[7,128,12288]{1,2,0:T(8,128)} fusion(f32[7,128,12288]{1,2,0:T(8,128)} %bitcast_dynamic-update-slice_fusion.2, f32[134,12288]{0,1:T(8,128)S(1)} %bitcast.210, f32[128,4096]{0,1:T(8,128)S(1)} %copy-done.2, f32[128,4096]{0,1:T(8,128)S(1)} %get-tuple-element.40, f32[128,4096]{0,1:T(8,128)S(1)} %copy-done.5), kind=kLoop, calls=%fused_computation.54 | loop fusion | flops 4718592 | bytes 18874368
  455.4 7.2 %bitcast_dynamic-update-slice_fusion = f32[7,128,12288]{1,2,0:T(8,128)} fusion(f32[7,128,12288]{1,2,0:T(8,128)} %bitcast_dynamic-update-slice_fusion.1, f32[134,12288]{0,1:T(8,128)S(1)} %bitcast.210, f32[128,4096]{0,1:T(8,128)S(1)} %copy-done.2, f32[128,4096]{0,1:T(8,128)S(1)} %get-tuple-element.40, f32[128,4096]{0,1:T(8,128)S(1)} %copy-done.5), kind=kLoop, calls=%fused_computation.53 | loop fusion | flops 4718592 | bytes 18874368 | tf_op jit(solution)/shard_map/stack | solution.py:164
  463.9 20.5 %reduce_sum.18 = bf16[7,12288]{1,0:T(8,128)(2,1)S(1)} reduce(f32[7,128,12288]{1,2,0:T(8,128)} %bitcast_dynamic-update-slice_fusion, f32[]{:T(128)} %constant.55.clone.1), dimensions={1}, to_apply=%region_0.1 | reduce | flops 10924032 | bytes 44212228 | tf_op jit(solution)/shard_map/reduce_sum | solution.py:163
  489.0 12.3 %pad_maximum_fusion = f32[134,12288]{0,1:T(8,128)} fusion(f32[6,12288]{0,1:T(8,128)} %copy.94, f32[128,4096]{0,1:T(8,128)} %get-tuple-element.41, f32[128,4096]{0,1:T(8,128)S(1)} %get-tuple-element.40, f32[128,4096]{0,1:T(8,128)} %copy-done.4), kind=kLoop, calls=%fused_computation | loop fusion | flops 4939776 | bytes 13172736 | tf_op jit(solution)/shard_map/concatenate | solution.py:156
  501.3 31.6 %fusion.46 = bf16[1,128,12288]{1,2,0:T(8,128)(2,1)} fusion(f32[134,12288]{0,1:T(8,128)} %pad_maximum_fusion, f32[12288]{0:T(1024)S(1)} %bitcast.244, f32[12288]{0:T(1024)S(1)} %bitcast.246, f32[12288]{0:T(1024)S(1)} %bitcast.236, f32[12288]{0:T(1024)S(1)} %bitcast.238, f32[12288]{0:T(1024)S(1)} %bitcast.240, f32[12288]{0:T(1024)S(1)} %bitcast.242, ...), kind=kLoop, calls=%fused_computation.89 | loop fusion | flops 25165824 | bytes 47529984 | tf_op jit(solution)/shard_map/broadcast_in_dim | solution.py:174
  537.5 68.2 %all-reduce.2.cloned.1.call-done = bf16[1,7,12288]{2,0,1:T(2,128)(2,1)} async-done(((bf16[1,7,12288]{2,0,1:T(2,128)(2,1)}), bf16[1,7,12288]{2,0,1:T(2,128)(2,1)}) %all-reduce.2.cloned.1.call-update) | async-done | bytes 172048 | tf_op jit(solution)/shard_map/psum | solution.py:173
  (147 shorter events, 180.2 us)
Async XLA Ops:
  7.2 14.5 %copy-start.29 = (f32[1,7,12288]{2,0,1:T(1,128)S(1)}, f32[1,7,12288]{2,0,1:T(1,128)}, u32[]{:S(2)}) copy-start(f32[1,7,12288]{2,0,1:T(1,128)} %param.7) | copy-start | bytes 1032196
  9.5 141.1 %collective-permute-start.2 = (bf16[1,128,4096]{1,2,0:T(8,128)(2,1)}, bf16[1,128,4096]{1,2,0:T(8,128)(2,1)S(1)}, u32[]{:S(2)}, u32[]{:S(2)}) collective-permute-start(bf16[1,128,4096]{1,2,0:T(8,128)(2,1)} %copy.84), channel_id=1, source_target_pairs={{0,112},{16,0},{32,16},{48,32},{64,48},{80,64},{96,80},{112,96},{1... | collective-permute-start | bytes 3145736 | tf_op jit(solution)/shard_map/ppermute | solution.py:11
  19.9 96.0 %copy-start.14 = (bf16[1,256,2048]{2,1,0:T(8,128)(2,1)S(1)}, bf16[1,256,2048]{2,1,0:T(8,128)(2,1)}, u32[]{:S(2)}) copy-start(bf16[1,256,2048]{2,1,0:T(8,128)(2,1)} %param.8) | copy-start | bytes 3145732
  19.9 84.7 %collective-permute-start = (bf16[1,128,12288]{1,2,0:T(8,128)(2,1)}, bf16[1,128,12288]{1,2,0:T(8,128)(2,1)}, u32[]{:S(2)}, u32[]{:S(2)}) collective-permute-start(bf16[1,128,12288]{1,2,0:T(8,128)(2,1)} %copy.69), channel_id=1, source_target_pairs={{0,16},{16,32},{32,48},{48,64},{64,80},{80,96},{96,112},{112,0},{1... | collective-permute-start | bytes 9437192 | tf_op jit(solution)/shard_map/ppermute | solution.py:11
  22.4 103.6 %copy-start.15 = (f32[1,1,12288]{2,0,1:T(1,128)}, f32[1,1,12288]{2,0,1:T(1,128)S(1)}, u32[]{:S(2)}) copy-start(f32[1,1,12288]{2,0,1:T(1,128)S(1)} %get-tuple-element.45) | copy-start | bytes 147460
  112.0 5.6 collective-permute-start.1
  126.0 24.6 %copy-start = (f32[134,12288]{0,1:T(8,128)}, f32[134,12288]{0,1:T(8,128)S(1)}, u32[]{:S(2)}) copy-start(f32[134,12288]{0,1:T(8,128)S(1)} %maximum_convert_fusion) | copy-start | bytes 19759108
  153.8 20.8 %all-to-all-start.2 = ((bf16[128,16,256]{0,2,1:T(8,128)(2,1)}), bf16[128,16,256]{0,2,1:T(8,128)(2,1)S(1)}, u32[]{:S(2)}, u32[]{:S(2)}) async-start(bf16[128,16,256]{0,2,1:T(8,128)(2,1)} %bitcast.232), calls=%async_computation.2 | async-start | bytes 2097152 | tf_op jit(solution)/shard_map/all_to_all | solution.py:141
  290.1 18.2 %slice-start.3 = ((s8[8388608]{0:T(1024)(128)(4,1)}), s8[4194304]{0:T(1024)(128)(4,1)S(1)}, s32[]{:S(2)}) async-start(s8[8388608]{0:T(1024)(128)(4,1)} %bitcast.211), calls=%async_computation.8 | async-start | bytes 8388608
  294.3 14.0 %slice-start.4 = ((s8[8388608]{0:T(1024)(128)(4,1)}), s8[4194304]{0:T(1024)(128)(4,1)S(1)}, s32[]{:S(2)}) async-start(s8[8388608]{0:T(1024)(128)(4,1)} %bitcast.211), calls=%async_computation.9 | async-start | bytes 8388608
  360.6 20.5 %all-to-all-start.1 = ((bf16[16,128,256]{2,1,0:T(8,128)(2,1)}), bf16[16,128,256]{2,1,0:T(8,128)(2,1)}, u32[]{:S(2)}, u32[]{:S(2)}) async-start(bf16[16,128,256]{2,1,0:T(8,128)(2,1)} %bitcast.231), calls=%async_computation.1 | async-start | bytes 2097152 | tf_op jit(solution)/shard_map/all_to_all | solution.py:140
  367.3 238.5 %all-reduce.2.cloned.1.call-start = ((), (), s32[]{:S(2)}) async-start(), calls=%async_computation.4 | async-start | bytes 688128 | tf_op jit(solution)/shard_map/psum | solution.py:173
  390.7 16.8 %copy-start.4 = (f32[128,4096]{0,1:T(8,128)}, f32[128,4096]{0,1:T(8,128)S(1)}, u32[]{:S(2)}) copy-start(f32[128,4096]{0,1:T(8,128)S(1)} %get-tuple-element.43) | copy-start | bytes 6291460
  410.7 74.7 %collective-permute-start.3 = (bf16[6,12288]{1,0:T(8,128)(2,1)S(1)}, bf16[6,12288]{1,0:T(8,128)(2,1)S(1)}, u32[]{:S(2)}, u32[]{:S(2)}) collective-permute-start(bf16[6,12288]{1,0:T(8,128)(2,1)S(1)} %copy.93), channel_id=1, source_target_pairs={{1,0},{2,1},{3,2},{4,3},{5,4},{6,5},{7,6},{8,7},{9,8},{10,9},{11,1... | collective-permute-start | bytes 442376 | tf_op jit(solution)/shard_map/ppermute | solution.py:17
  412.9 20.3 %slice-start = ((s8[12582912]{0:T(1024)(128)(4,1)}), s8[4194304]{0:T(1024)(128)(4,1)S(1)}, s32[]{:S(2)}) async-start(s8[12582912]{0:T(1024)(128)(4,1)} %bitcast.209), calls=%async_computation.5 | async-start | bytes 8388608
  412.9 20.3 %slice-start.1 = ((s8[12582912]{0:T(1024)(128)(4,1)}), s8[4194304]{0:T(1024)(128)(4,1)S(1)}, s32[]{:S(2)}) async-start(s8[12582912]{0:T(1024)(128)(4,1)} %bitcast.209), calls=%async_computation.6 | async-start | bytes 8388608
  488.9 12.3 %copy-start.6 = (f32[128,4096]{0,1:T(8,128)S(1)}, f32[128,4096]{0,1:T(8,128)}, u32[]{:S(2)}) copy-start(f32[128,4096]{0,1:T(8,128)} %copy-done.4) | copy-start | bytes 6291460
  488.9 12.3 %copy-start.16 = (f32[1,1,12288]{2,0,1:T(1,128)S(1)}, f32[1,1,12288]{2,0,1:T(1,128)}, u32[]{:S(2)}) copy-start(f32[1,1,12288]{2,0,1:T(1,128)} %copy-done.15) | copy-start | bytes 147460
  488.9 12.3 %copy-start.18 = (f32[1,1,12288]{2,0,1:T(1,128)S(1)}, f32[1,1,12288]{2,0,1:T(1,128)}, u32[]{:S(2)}) copy-start(f32[1,1,12288]{2,0,1:T(1,128)} %get-tuple-element.46) | copy-start | bytes 147460
  488.9 12.3 %copy-start.20 = (f32[1,1,12288]{2,0,1:T(1,128)S(1)}, f32[1,1,12288]{2,0,1:T(1,128)}, u32[]{:S(2)}) copy-start(f32[1,1,12288]{2,0,1:T(1,128)} %get-tuple-element.47) | copy-start | bytes 147460
  488.9 12.3 %copy-start.22 = (f32[1,1,12288]{2,0,1:T(1,128)S(1)}, f32[1,1,12288]{2,0,1:T(1,128)}, u32[]{:S(2)}) copy-start(f32[1,1,12288]{2,0,1:T(1,128)} %get-tuple-element.48) | copy-start | bytes 147460
  488.9 12.3 %copy-start.24 = (f32[1,1,12288]{2,0,1:T(1,128)S(1)}, f32[1,1,12288]{2,0,1:T(1,128)}, u32[]{:S(2)}) copy-start(f32[1,1,12288]{2,0,1:T(1,128)} %get-tuple-element.49) | copy-start | bytes 147460
  488.9 12.3 %copy-start.26 = (f32[1,1,12288]{2,0,1:T(1,128)S(1)}, f32[1,1,12288]{2,0,1:T(1,128)}, u32[]{:S(2)}) copy-start(f32[1,1,12288]{2,0,1:T(1,128)} %get-tuple-element.50) | copy-start | bytes 147460
  488.9 12.3 %copy-start.28 = (f32[1,1,12288]{2,0,1:T(1,128)S(1)}, f32[1,1,12288]{2,0,1:T(1,128)}, u32[]{:S(2)}) copy-start(f32[1,1,12288]{2,0,1:T(1,128)} %get-tuple-element.51) | copy-start | bytes 147460
  (22 other events, 144.2 us)
Sparse Core Ops, SparseCore 0:
  485.5 120.2 all-reduce.1
where the time goes:
time: 625 us; the launch traced here: 615 us
  other arithmetic  228 us (36%)
  waiting for transfers between devices  160 us (26%)
  matrix products  76.2 us (12%)
  local copies, waits for them, and re-layouts  72.4 us (12%)
  blocking collectives  39.5 us (6%)
  starting transfers between devices  24.3 us (4%)
  between operations  14.9 us (2%)
    ppermute x2, waiting for transfers between devices, passed_along(): return lax.ppermute(value, axis, pairs)  82.2 us
    psum x1, waiting for transfers between devices, on_device(): lax.psum(partial_kern.astype(jnp.bfloat16), 'ctx').astype(jnp.float32)  68.2 us
    dot_general x9, matrix products, contract(): return jnp.einsum(form, table, values, precision=lax.Precision.HIGH)  63.9 us
    unnamed x9, other arithmetic  52.6 us
    broadcast_in_dim x1, other arithmetic, on_device(): input_grad[None]  31.6 us
    add x1, other arithmetic, on_device(): sum((weights[offset][None, :] * padded[margin - offset:margin - offset +...  24.5 us
    reduce_sum x1, other arithmetic, on_device(): jnp.sum(jnp.stack([feat_grad * padded[margin - offset:margin - offset + t...  20.5 us
    all_to_all x1, blocking collectives, on_device(): lax.all_to_all(gated, 'ctx', split_axis=1, concat_axis=0, tiled=True)  20.2 us
  transfers between devices with their start and end apart: 7, of which 5 were waited for; matrix products, arithmetic and copies ran while one was open for 31% of the time, Pallas kernels for 0%

commit v1 on v0

--- a/solution.py
+++ b/solution.py
@@ -132,7 +132,9 @@
     filt_spec = forward_transform(filt[0].T, tables)
     grad_in = incoming.astype(jnp.float32)
     grad_mix = (grad_in * query).astype(jnp.bfloat16)
-    gated_part = lax.all_to_all(gated, "ctx", split_axis=1, concat_axis=0, tiled=True)
+    gated_part = jnp.concatenate(
+        lax.all_to_all(jnp.stack(jnp.split(gated, lax.axis_size("ctx"), 1), 0), "ctx", 0, 0), 0
+    )
     gated_f = gated_part.astype(jnp.float32)
     gated_spec = forward_transform(gated_part, tables)
     mixed = inverse_transform(cmul(gated_spec, filt_spec, False), tables)

time: 625 us -> 529 us (0.85)
  other arithmetic: 228 us -> 117 us
  waiting for transfers between devices: 160 us -> 206 us
  local copies, waits for them, and re-layouts: 72.4 us -> 44.7 us
    psum x1, waiting for transfers between devices: 68.2 us -> 108 us  [on_device(): lax.psum(partial_kern.astype(jnp.bfloat16), 'ctx').astype(jnp.float32)]
    unnamed x9 -> x10, other arithmetic: 52.6 us -> 19.7 us
    broadcast_in_dim x1, other arithmetic: 31.6 us -> 7.59 us  [on_device(): input_grad[None]]
    add x1, other arithmetic: 24.5 us -> 5.15 us  [on_device(): sum((weights[offset][None, :] * padded[margin - offset:margin - offset +...]
    concatenate x1, other arithmetic: 12.3 us -> 2.82 us  [on_device(): extended = jnp.concatenate([feat_grad, after], axis=0)]
    unnamed x84 -> x83, local copies, waits for them, and re-layouts: 19.6 us -> 10.2 us
    slice x2 -> x1, local copies, waits for them, and re-layouts: 7.43 us -> 0.97 us  [on_device(): before = from_behind(source[tokens_dev - margin:], 'ctx', 1)]
    concatenate x1, other arithmetic: 6.71 us -> 0.34 us  [on_device(): jnp.concatenate([grad_in * inner, through_f * value, through_f * keyed],...]
  transfers between devices with their start and end apart: 7 -> 7, of which waited for: 5 -> 5; matrix products, arithmetic and copies ran while one was open for 31% -> 15% of each run, Pallas kernels for 0% -> 0%
where the time goes in v1:
time: 529 us; the launch traced here: 520 us
  waiting for transfers between devices  206 us (39%)
  other arithmetic  117 us (22%)
  matrix products  74.6 us (14%)
  local copies, waits for them, and re-layouts  44.7 us (8%)
  blocking collectives  38.7 us (7%)
  starting transfers between devices  24.1 us (5%)
  between operations  15 us (3%)
    psum x1, waiting for transfers between devices, on_device(): lax.psum(partial_kern.astype(jnp.bfloat16), 'ctx').astype(jnp.float32)  108 us
    ppermute x2, waiting for transfers between devices, passed_along(): return lax.ppermute(value, axis, pairs)  87.7 us
    dot_general x9, matrix products, contract(): return jnp.einsum(form, table, values, precision=lax.Precision.HIGH)  63.6 us
    unnamed x10, other arithmetic  19.7 us
    all_to_all x1, blocking collectives, on_device(): lax.all_to_all(through_part, 'ctx', split_axis=0, concat_axis=1, tiled=True)  19.4 us
    all_to_all x1, blocking collectives, on_device(): lax.all_to_all(jnp.stack(jnp.split(gated, lax.axis_size('ctx'), 1), 0), '...  19.3 us
    dot_general x3, local copies, waits for them, and re-layouts, contract(): return jnp.einsum(form, table, values, precision=lax.Precision.HIGH)  17.9 us
    reduce_sum x1, other arithmetic, on_device(): jnp.sum(jnp.stack([feat_grad * padded[margin - offset:margin - offset + t...  16 us
  transfers between devices with their start and end apart: 7, of which 5 were waited for; matrix products, arithmetic and copies ran while one was open for 15% of the time, Pallas kernels for 0%

profile of v1, /device:TPU:25, one launch (start us, length us, event | category | flops | bytes accessed | tf_op | source)
XLA Modules:
  0.0 520.1 jit_solution(9017665727570421674)
XLA Ops:
  7.2 5.9 %collective-permute-start.2 = (bf16[1,128,4096]{2,1,0:T(8,128)(2,1)}, bf16[1,128,4096]{2,1,0:T(8,128)(2,1)S(1)}, u32[]{:S(2)}, u32[]{:S(2)}) collective-permute-start(bf16[1,128,4096]{2,1,0:T(8,128)(2,1)} %param.6), channel_id=1, source_target_pairs={{0,112},{16,0},{32,16},{48,32},{64,48},{80,64},{96,80},{112,96},{1... | collective-permute-start | bytes 3145736 | tf_op jit(solution)/shard_map/ppermute | solution.py:11
  14.6 87.7 %collective-permute-done = bf16[1,128,12288]{2,1,0:T(8,128)(2,1)} collective-permute-done((bf16[1,128,12288]{2,1,0:T(8,128)(2,1)}, bf16[1,128,12288]{2,1,0:T(8,128)(2,1)}, u32[]{:S(2)}, u32[]{:S(2)}) %collective-permute-start) | collective-permute-done | bytes 3145760 | tf_op jit(solution)/shard_map/ppermute | solution.py:11
  111.5 5.2 multiply_add_fusion
  123.6 7.0 %all-to-all-start.2 = ((bf16[128,16,256]{2,0,1:T(8,128)(2,1)}), bf16[128,16,256]{2,0,1:T(8,128)(2,1)S(1)}, u32[]{:S(2)}, u32[]{:S(2)}) async-start(bf16[128,16,256]{2,0,1:T(8,128)(2,1)} %copy.58), calls=%async_computation.2 | async-start | bytes 2097152 | tf_op jit(solution)/shard_map/all_to_all | solution.py:143
  136.5 7.9 %all-to-all-done.2 = bf16[128,16,256]{2,0,1:T(8,128)(2,1)S(1)} async-done(((bf16[128,16,256]{2,0,1:T(8,128)(2,1)}), bf16[128,16,256]{2,0,1:T(8,128)(2,1)S(1)}, u32[]{:S(2)}, u32[]{:S(2)}) %all-to-all-start.2) | async-done | bytes 1048608 | tf_op jit(solution)/shard_map/all_to_all | solution.py:143
  148.1 7.0 %multiply_add_fusion.5 = (f32[1,64,64,256]{3,1,2,0:T(8,128)}, f32[1,64,64,256]{3,1,2,0:T(8,128)}, f32[1,64,64,256]{3,1,2,0:T(8,128)}, f32[1,64,64,256]{3,1,2,0:T(8,128)}) fusion(f32[2,64,64,256]{3,1,2,0:T(8,128)S(1)} %convolution_add_fusion, f32[64,64]{0,1:T(8,128)S(1)} %get-tuple-element.59, f32[64,64]{0,1:T(8,128)S(1)} %get-tuple-element.60, ...), kind=kLoop, calls=%fused_computation.68 | loop fusion | flops 12582912 | bytes 33587200 | tf_op jit(solution)/shard_map/add | solution.py:77
  162.7 8.5 %fusion.40 = f32[2,64,64,256]{3,2,0,1:T(8,128)S(1)} fusion(f32[2,64,64,256,1]{3,1,2,0,4:T(8,128)S(1)} %maximum_bitcast_fusion.4, f32[1,64,2,64]{3,1,2,0:T(8,128)S(1)} %get-tuple-element.52, f32[1,64,2,64]{3,1,2,0:T(8,128)S(1)} %get-tuple-element.55), kind=kOutput, calls=%fused_computation.83 | convolution fusion | flops 1610629120 | bytes 16842752 | tf_op jit(solution)/shard_map/pqsj,skjc->pkqc/dot_general | solution.py:58
  171.2 8.7 %fusion.37 = f32[2,64,64,256]{3,2,0,1:T(8,128)S(1)} fusion(f32[2,64,64,256,1]{3,1,2,0,4:T(8,128)S(1)} %maximum_bitcast_fusion.1, f32[1,64,2,64]{3,1,2,0:T(8,128)S(1)} %get-tuple-element.52, f32[1,64,2,64]{3,1,2,0:T(8,128)S(1)} %get-tuple-element.55), kind=kOutput, calls=%fused_computation.82 | convolution fusion | flops 1610629120 | bytes 16842752 | tf_op jit(solution)/shard_map/pqsj,skjc->pkqc/dot_general | solution.py:58
  184.5 6.1 %fusion.44 = f32[64,256,2,64]{1,3,2,0:T(8,128)S(1)} fusion(f32[1,64,64,256]{3,2,0,1:T(8,128)} %get-tuple-element.18, f32[1,64,64,256]{3,2,0,1:T(8,128)S(1)} %get-tuple-element.17, f32[1,64,2,64]{3,1,2,0:T(8,128)S(1)} %get-tuple-element.56, f32[1,64,2,64]{3,1,2,0:T(8,128)S(1)} %get-tuple-element.51), kind=kOutput, calls=%fused_computation.85 | convolution fusion | flops 1612726272 | bytes 16842752 | tf_op jit(solution)/shard_map/pjsq,skqc->pkjc/dot_general | solution.py:58
  190.6 4.9 copy.136
  202.1 19.4 %all_to_all.41 = bf16[16,128,256]{2,1,0:T(8,128)(2,1)S(1)} all-to-all(bf16[16,128,256]{2,1,0:T(8,128)(2,1)S(1)} %fusion.48), channel_id=1, replica_groups=mesh['section'=8,'ctx'=16] {'ctx'}, dimensions={0} | all-to-all | bytes 2097152 | tf_op jit(solution)/shard_map/all_to_all | solution.py:152
  231.4 19.3 %all_to_all.42 = bf16[16,128,256]{2,1,0:T(8,128)(2,1)S(1)} all-to-all(bf16[16,128,256]{2,1,0:T(8,128)(2,1)S(1)} %fusion.78), channel_id=1, replica_groups=mesh['section'=8,'ctx'=16] {'ctx'}, dimensions={0} | all-to-all | bytes 2097152 | tf_op jit(solution)/shard_map/all_to_all | solution.py:136
  258.9 14.0 %fusion.34 = f32[2,64,64,256]{3,2,0,1:T(8,128)} fusion(f32[2,64,64,256,1]{3,1,2,0,4:T(8,128)} %maximum_bitcast_fusion, f32[1,64,2,64]{3,1,2,0:T(8,128)S(1)} %get-tuple-element.52, f32[1,64,2,64]{3,1,2,0:T(8,128)S(1)} %get-tuple-element.55), kind=kOutput, calls=%fused_computation.81 | convolution fusion | flops 1610629120 | bytes 16842752 | tf_op jit(solution)/shard_map/pqsj,skjc->pkqc/dot_general | solution.py:58
  272.8 11.9 %multiply_add_fusion.2 = (f32[1,64,64,256]{3,2,0,1:T(8,128)}, f32[1,64,64,256]{3,2,0,1:T(8,128)}, f32[1,64,64,256]{3,2,0,1:T(8,128)}, f32[1,64,64,256]{3,2,0,1:T(8,128)}) fusion(f32[2,64,64,256]{3,2,0,1:T(8,128)S(1)} %bitcast.270, f32[2,64,64,256]{3,2,0,1:T(8,128)} %fusion.34, f32[2,64,64,256]{3,2,0,1:T(8,128)} %copy-done.4), kind=kLoop, calls=%fused_computation.62 | loop fusion | flops 12582912 | bytes 41943040 | tf_op jit(solution)/shard_map/add | solution.py:86
  284.8 6.5 %fusion.45 = f32[64,256,2,64]{1,3,2,0:T(8,128)S(1)} fusion(f32[1,64,64,256]{3,2,0,1:T(8,128)} %get-tuple-element.33, f32[1,64,64,256]{3,2,0,1:T(8,128)} %get-tuple-element.34, f32[1,64,2,64]{3,1,2,0:T(8,128)S(1)} %get-tuple-element.56, f32[1,64,2,64]{3,1,2,0:T(8,128)S(1)} %get-tuple-element.51), kind=kOutput, calls=%fused_computation.86 | convolution fusion | flops 1612726272 | bytes 16842752 | tf_op jit(solution)/shard_map/pjsq,skqc->pkjc/dot_general | solution.py:58
  296.1 6.7 %fusion.43 = f32[64,256,2,64]{1,3,2,0:T(8,128)S(1)} fusion(f32[1,64,64,256]{3,2,0,1:T(8,128)} %get-tuple-element.16, f32[1,64,64,256]{3,2,0,1:T(8,128)} %get-tuple-element.15, f32[1,64,2,64]{3,1,2,0:T(8,128)S(1)} %get-tuple-element.56, f32[1,64,2,64]{3,1,2,0:T(8,128)S(1)} %get-tuple-element.51), kind=kOutput, calls=%fused_computation.84 | convolution fusion | flops 1612726272 | bytes 16842752 | tf_op jit(solution)/shard_map/pjsq,skqc->pkjc/dot_general | solution.py:58
  302.8 8.2 %copy.135 = f32[64,256,2,64]{1,0,3,2:T(8,128)} copy(f32[64,256,2,64]{1,3,2,0:T(8,128)S(1)} %fusion.43) | data formatting | bytes 16777216 | tf_op jit(solution)/shard_map/pjsq,skqc->pkjc/dot_general | solution.py:58
  310.9 7.7 %multiply_subtract_fusion = (f32[1,64,64,256]{3,1,2,0:T(8,128)}, f32[1,64,64,256]{3,1,2,0:T(8,128)}, f32[1,64,64,256]{3,1,2,0:T(8,128)S(1)}, f32[1,64,64,256]{3,1,2,0:T(8,128)}) fusion(f32[2,64,64,256]{3,1,2,0:T(8,128)} %bitcast.275, f32[64,64]{0,1:T(8,128)S(1)} %get-tuple-element.59, f32[64,64]{0,1:T(8,128)S(1)} %get-tuple-element.60, ...), kind=kLoop, calls=%fused_computation.60 | loop fusion | flops 12582912 | bytes 33587200 | tf_op jit(solution)/shard_map/sub | solution.py:99
  318.7 5.1 fusion.51
  325.4 6.6 %all-to-all-start.1 = ((bf16[16,128,256]{2,1,0:T(8,128)(2,1)}), bf16[16,128,256]{2,1,0:T(8,128)(2,1)}, u32[]{:S(2)}, u32[]{:S(2)}) async-start(bf16[16,128,256]{2,1,0:T(8,128)(2,1)} %bitcast.286), calls=%async_computation.1 | async-start | bytes 2097152 | tf_op jit(solution)/shard_map/all_to_all | solution.py:142
  332.0 5.1 bitcast_multiply_fusion
  375.3 16.0 %reduce_sum.18 = bf16[7,12288]{1,0:T(8,128)(2,1)S(1)} reduce(f32[7,128,12288]{2,1,0:T(8,128)} %bitcast_dynamic-update-slice_fusion, f32[]{:T(128)} %constant.55.clone.1), dimensions={1}, to_apply=%region_0.1 | reduce | flops 10924032 | bytes 44212228 | tf_op jit(solution)/shard_map/reduce_sum | solution.py:165
  395.2 7.6 %fusion.46 = bf16[1,128,12288]{2,1,0:T(8,128)(2,1)} fusion(f32[134,12288]{1,0:T(8,128)S(1)} %pad_maximum_fusion, f32[12288]{0:T(1024)S(1)} %bitcast.299, f32[12288]{0:T(1024)S(1)} %bitcast.301, f32[12288]{0:T(1024)S(1)} %bitcast.291, f32[12288]{0:T(1024)S(1)} %bitcast.293, f32[12288]{0:T(1024)S(1)} %bitcast.295, f32[12288]{0:T(1024)S(1)} %bitcast.297, ...), kind=kLoop, calls=%fused_computation.87 | loop fusion | flops 25165824 | bytes 47529984 | tf_op jit(solution)/shard_map/broadcast_in_dim | solution.py:176
  402.8 108.2 %all-reduce.2.cloned.1.call-done = bf16[1,7,12288]{2,0,1:T(2,128)(2,1)} async-done(((bf16[1,7,12288]{2,0,1:T(2,128)(2,1)}), bf16[1,7,12288]{2,0,1:T(2,128)(2,1)}) %all-reduce.2.cloned.1.call-update) | async-done | bytes 172048 | tf_op jit(solution)/shard_map/psum | solution.py:175
  (147 shorter events, 114.2 us)
Async XLA Ops:
  7.2 109.5 %collective-permute-start.2 = (bf16[1,128,4096]{2,1,0:T(8,128)(2,1)}, bf16[1,128,4096]{2,1,0:T(8,128)(2,1)S(1)}, u32[]{:S(2)}, u32[]{:S(2)}) collective-permute-start(bf16[1,128,4096]{2,1,0:T(8,128)(2,1)} %param.6), channel_id=1, source_target_pairs={{0,112},{16,0},{32,16},{48,32},{64,48},{80,64},{96,80},{112,96},{1... | collective-permute-start | bytes 3145736 | tf_op jit(solution)/shard_map/ppermute | solution.py:11
  13.0 89.3 %collective-permute-start = (bf16[1,128,12288]{2,1,0:T(8,128)(2,1)}, bf16[1,128,12288]{2,1,0:T(8,128)(2,1)}, u32[]{:S(2)}, u32[]{:S(2)}) collective-permute-start(bf16[1,128,12288]{2,1,0:T(8,128)(2,1)} %param.5), channel_id=1, source_target_pairs={{0,16},{16,32},{32,48},{48,64},{64,80},{80,96},{96,112},{112,0},{1... | collective-permute-start | bytes 9437192 | tf_op jit(solution)/shard_map/ppermute | solution.py:11
  14.5 96.9 %copy-start.12 = (f32[1,1,12288]{2,0,1:T(1,128)}, f32[1,1,12288]{2,0,1:T(1,128)S(1)}, u32[]{:S(2)}) copy-start(f32[1,1,12288]{2,0,1:T(1,128)S(1)} %get-tuple-element.40) | copy-start | bytes 147460
  14.5 96.9 %copy-start.14 = (f32[1,1,12288]{2,0,1:T(1,128)}, f32[1,1,12288]{2,0,1:T(1,128)S(1)}, u32[]{:S(2)}) copy-start(f32[1,1,12288]{2,0,1:T(1,128)S(1)} %get-tuple-element.41) | copy-start | bytes 147460
  14.6 96.9 %copy-start.16 = (f32[1,1,12288]{2,0,1:T(1,128)}, f32[1,1,12288]{2,0,1:T(1,128)S(1)}, u32[]{:S(2)}) copy-start(f32[1,1,12288]{2,0,1:T(1,128)S(1)} %get-tuple-element.42) | copy-start | bytes 147460
  14.6 96.9 %copy-start.18 = (f32[1,1,12288]{2,0,1:T(1,128)}, f32[1,1,12288]{2,0,1:T(1,128)S(1)}, u32[]{:S(2)}) copy-start(f32[1,1,12288]{2,0,1:T(1,128)S(1)} %get-tuple-element.43) | copy-start | bytes 147460
  14.6 96.9 %copy-start.20 = (f32[1,1,12288]{2,0,1:T(1,128)}, f32[1,1,12288]{2,0,1:T(1,128)S(1)}, u32[]{:S(2)}) copy-start(f32[1,1,12288]{2,0,1:T(1,128)S(1)} %get-tuple-element.44) | copy-start | bytes 147460
  14.6 96.9 %copy-start.22 = (f32[1,1,12288]{2,0,1:T(1,128)}, f32[1,1,12288]{2,0,1:T(1,128)S(1)}, u32[]{:S(2)}) copy-start(f32[1,1,12288]{2,0,1:T(1,128)S(1)} %get-tuple-element.45) | copy-start | bytes 147460
  14.6 96.9 %copy-start.24 = (f32[1,1,12288]{2,0,1:T(1,128)}, f32[1,1,12288]{2,0,1:T(1,128)S(1)}, u32[]{:S(2)}) copy-start(f32[1,1,12288]{2,0,1:T(1,128)S(1)} %get-tuple-element.46) | copy-start | bytes 147460
  103.3 5.3 %collective-permute-start.1 = (bf16[6,12288]{1,0:T(8,128)(2,1)S(1)}, bf16[6,12288]{1,0:T(8,128)(2,1)S(1)}, u32[]{:S(2)}, u32[]{:S(2)}) collective-permute-start(bf16[6,12288]{1,0:T(8,128)(2,1)S(1)} %slice_bitcast_fusion), channel_id=1, source_target_pairs={{0,1},{1,2},{2,3},{3,4},{4,5},{5,6},{6,7},{7,8},{8,9},{9,10},{10,1... | collective-permute-start | bytes 442376 | tf_op jit(solution)/shard_map/ppermute | solution.py:17
  111.4 5.2 %copy-start = (f32[134,12288]{1,0:T(8,128)}, f32[134,12288]{1,0:T(8,128)S(1)}, u32[]{:S(2)}) copy-start(f32[134,12288]{1,0:T(8,128)S(1)} %maximum_convert_fusion) | copy-start | bytes 19759108
  119.3 12.5 %copy-start.10 = (bf16[1,128,4096]{2,1,0:T(8,128)(2,1)}, bf16[1,128,4096]{2,1,0:T(8,128)(2,1)S(1)}, u32[]{:S(2)}) copy-start(bf16[1,128,4096]{2,1,0:T(8,128)(2,1)S(1)} %collective-permute-done.2) | copy-start | bytes 3145732
  123.6 20.8 %all-to-all-start.2 = ((bf16[128,16,256]{2,0,1:T(8,128)(2,1)}), bf16[128,16,256]{2,0,1:T(8,128)(2,1)S(1)}, u32[]{:S(2)}, u32[]{:S(2)}) async-start(bf16[128,16,256]{2,0,1:T(8,128)(2,1)} %copy.58), calls=%async_computation.2 | async-start | bytes 2097152 | tf_op jit(solution)/shard_map/all_to_all | solution.py:143
  155.0 4.6 copy-start.7
  171.2 8.7 %copy-start.3 = (f32[2,64,64,256]{3,2,0,1:T(8,128)}, f32[2,64,64,256]{3,2,0,1:T(8,128)S(1)}, u32[]{:S(2)}) copy-start(f32[2,64,64,256]{3,2,0,1:T(8,128)S(1)} %fusion.40) | copy-start | bytes 25165828
  179.9 4.6 copy-start.4
  231.1 19.6 %copy-start.8 = (bf16[128,4096]{1,0:T(8,128)(2,1)}, bf16[128,4096]{1,0:T(8,128)(2,1)S(1)}, u32[]{:S(2)}) copy-start(bf16[128,4096]{1,0:T(8,128)(2,1)S(1)} %get-tuple-element.37) | copy-start | bytes 3145732
  254.7 18.1 %slice-start.2 = ((s8[8388608]{0:T(1024)(128)(4,1)}), s8[4194304]{0:T(1024)(128)(4,1)S(1)}, s32[]{:S(2)}) async-start(s8[8388608]{0:T(1024)(128)(4,1)} %bitcast.269), calls=%async_computation.7 | async-start | bytes 8388608
  258.9 14.0 %slice-start.3 = ((s8[8388608]{0:T(1024)(128)(4,1)}), s8[4194304]{0:T(1024)(128)(4,1)S(1)}, s32[]{:S(2)}) async-start(s8[8388608]{0:T(1024)(128)(4,1)} %bitcast.269), calls=%async_computation.8 | async-start | bytes 8388608
  325.4 20.6 %all-to-all-start.1 = ((bf16[16,128,256]{2,1,0:T(8,128)(2,1)}), bf16[16,128,256]{2,1,0:T(8,128)(2,1)}, u32[]{:S(2)}, u32[]{:S(2)}) async-start(bf16[16,128,256]{2,1,0:T(8,128)(2,1)} %bitcast.286), calls=%async_computation.1 | async-start | bytes 2097152 | tf_op jit(solution)/shard_map/all_to_all | solution.py:142
  332.0 179.0 %all-reduce.2.cloned.1.call-start = ((), (), s32[]{:S(2)}) async-start(), calls=%async_computation.4 | async-start | bytes 688128 | tf_op jit(solution)/shard_map/psum | solution.py:175
  339.6 8.1 %copy-start.26 = (f32[1,4096]{1,0:T(1,128)S(1)}, f32[1,4096]{1,0:T(1,128)}, u32[]{:S(2)}) copy-start(f32[1,4096]{1,0:T(1,128)} %param.9) | copy-start | bytes 49156
  351.0 21.2 %copy-start.2 = (f32[128,4096]{1,0:T(8,128)}, f32[128,4096]{1,0:T(8,128)S(1)}, u32[]{:S(2)}) copy-start(f32[128,4096]{1,0:T(8,128)S(1)} %get-tuple-element.38) | copy-start | bytes 6291460
  355.2 37.0 %collective-permute-start.3 = (bf16[6,12288]{1,0:T(8,128)(2,1)S(1)}, bf16[6,12288]{1,0:T(8,128)(2,1)S(1)}, u32[]{:S(2)}, u32[]{:S(2)}) collective-permute-start(bf16[6,12288]{1,0:T(8,128)(2,1)S(1)} %slice.372), channel_id=1, source_target_pairs={{1,0},{2,1},{3,2},{4,3},{5,4},{6,5},{7,6},{8,7},{9,8},{10,9},{11,1... | collective-permute-start | bytes 442376 | tf_op jit(solution)/shard_map/ppermute | solution.py:17
  (16 other events, 47.1 us)
Sparse Core Ops, SparseCore 0:
  392.3 118.6 all-reduce.1
